TPU v7x, 128 devices: a whole 4x4x4 slice. The times are simulated.
128 devices in a mesh: grp: 4 (over y), dev: 32 (over z, x, core).
Axes of the slice: x: 4, y: 4, z: 4, core: 2. Of those that a mesh axis runs over, the one named last changes fastest.
Arguments:
- integral_slabs: bfloat16 [32, 512, 512], P('dev'), may hold values from -6 to 6
- slab_owner: int32 [32], replicated, may hold values from 0 to 31, each once
- pair_orbs: int32 [1024, 2], P(('grp', 'dev')), may hold values from 0 to 31, all different within a row; in each aligned block of 8 rows (0 to 7, 8 to 15, ...) at most 2 rows name the same one
- domain_bases: bfloat16 [1024, 512, 128], P(('grp', 'dev')), may hold values from -0.25 to 0.25
- amplitudes: bfloat16 [1024, 128, 128], P(('grp', 'dev')), may hold values from -6 to 6
- coupled: int32 [1024, 32], P(('grp', 'dev')), may hold values from 0 to 31
- coupled_len: int32 [1024], P(('grp', 'dev')), may hold values from 1 to 32, as said below
Outputs:
- residual: float32 [1024, 128, 128], P(('grp', 'dev'))
Inputs may be any that keep to these rules, and one draw needn't show every extreme that they name: `slab_owner`: a permutation of the positions. `pair_orbs`: the two orbitals of a pair differ; among the pairs of one device no orbital is named more than 2 times. `coupled_len`: pair 0 uses all 32 slots.
All inputs are finite; a program needn't handle non-finite values.
Results may differ from a plain program's by a relative error of at most 0.005.
Values may be sent and summed in bfloat16 or wider, within the bound.
A program may use at most 128 MiB of HBM per device.

v0:
```python
import math

import jax
import jax.numpy as jnp
from jax import lax
from jax.sharding import PartitionSpec as P

NAUX = 512
NORB = 512
NPNO = 128


def side_positions(orbitals, slab_owner):
    flat = orbitals.reshape(-1)
    table = jnp.arange(slab_owner.shape[0], dtype=jnp.int32)
    return jnp.sum(jnp.where(flat[:, None] == table[None, :], slab_owner[None, :], 0), axis=1)


def make_fold(positions, slab_piece):
    rows = jnp.arange(slab_piece.shape[0], dtype=jnp.int32)
    select = (positions[:, None] == rows[None, :]).astype(jnp.bfloat16)
    picked = jnp.einsum("sk,kxn->sxn", select, slab_piece, preferred_element_type=jnp.float32)
    return picked.astype(jnp.bfloat16)


def half_pairs(halves):
    pair_count = halves.shape[0] // 2
    paired = halves.reshape(pair_count, 2, halves.shape[1], halves.shape[2])
    inverse_root = 1.0 / math.sqrt(NAUX)
    return (
        jnp.einsum("pan,pam->pnm", paired[:, 0], paired[:, 1], preferred_element_type=jnp.float32)
        * inverse_root
    )


def coupled_part(domain_bases, coupled, coupled_len, cand_bases, cand_amps):
    cand_count = cand_bases.shape[0]
    slot_live = (jnp.arange(coupled.shape[1])[None, :] < coupled_len[:, None]).astype(jnp.float32)
    matches = (
        coupled[:, :, None] == jnp.arange(cand_count, dtype=jnp.int32)[None, None, :]
    ).astype(jnp.float32)
    counts = jnp.einsum("ps,psc->pc", slot_live, matches)

    def one_pair(inputs):
        domain_basis, weights = inputs
        intersection = jnp.einsum(
            "ra,crb->cab", domain_basis, cand_bases, preferred_element_type=jnp.float32
        ).astype(jnp.bfloat16)
        projected = jnp.einsum(
            "cab,cbd->cad", intersection, cand_amps, preferred_element_type=jnp.float32
        ).astype(jnp.bfloat16)
        coupled_terms = jnp.einsum(
            "cad,ced->cae", projected, intersection, preferred_element_type=jnp.float32
        )
        return jnp.einsum("c,cae->ae", weights, coupled_terms)

    return lax.map(one_pair, (domain_bases, counts))


def on_device(
    integral_slabs, slab_owner, pair_orbs, domain_bases, amplitudes, coupled, coupled_len
):
    naux_full = integral_slabs.shape[1]
    norb_full = integral_slabs.shape[2]
    npno = domain_bases.shape[2]
    pair_count = domain_bases.shape[0]
    cand_bases, cand_amps = (
        lax.all_gather(domain_bases, "grp", axis=0, tiled=True),
        lax.all_gather(amplitudes, "grp", axis=0, tiled=True),
    )
    positions = side_positions(pair_orbs, slab_owner)
    side_slabs = make_fold(positions, lax.all_gather(integral_slabs, "dev", axis=0, tiled=True))
    paired_slabs = side_slabs.reshape(pair_count, 2, naux_full, norb_full)
    halves = jnp.einsum(
        "pkxn,pnq->pkxq", paired_slabs, domain_bases, preferred_element_type=jnp.float32
    ).astype(jnp.bfloat16)
    halves = halves.reshape(2 * pair_count, naux_full, npno)
    exchange = half_pairs(halves)
    coupled_sum = coupled_part(domain_bases, coupled, coupled_len, cand_bases, cand_amps)
    return exchange + NORB / NPNO * coupled_sum


def solution(mesh):
    in_specs = (
        P("dev", None, None),
        P(),
        P(("grp", "dev"), None),
        P(("grp", "dev"), None, None),
        P(("grp", "dev"), None, None),
        P(("grp", "dev"), None),
        P(("grp", "dev")),
    )
    out_specs = P(("grp", "dev"), None, None)
    return jax.shard_map(
        on_device, mesh=mesh, in_specs=in_specs, out_specs=out_specs, check_vma=False
    )
```

profile of v0, /device:TPU:1, one launch (start us, length us, event | category | flops | bytes accessed | tf_op | source)
XLA Modules:
  0.0 207.8 jit_solution(17346117150356649458)
XLA Ops:
  12.1 22.2 %all-gather.8.cloned.1.call-done = bf16[32,128,128]{2,1,0:T(8,128)(2,1)} async-done(((bf16[8,128,128]{2,1,0:T(8,128)(2,1)}), bf16[32,128,128]{2,1,0:T(8,128)(2,1)}) %all-gather.8.cloned.1.call-update) | async-done | bytes 1048592 | tf_op jit(solution)/shard_map/all_gather | solution.py:69
  34.3 52.2 %all-gather.6.cloned.1.call-done = bf16[32,512,128]{2,1,0:T(8,128)(2,1)} async-done(((bf16[8,512,128]{2,1,0:T(8,128)(2,1)}), bf16[32,512,128]{2,1,0:T(8,128)(2,1)}) %all-gather.6.cloned.1.call-update) | async-done | bytes 4194320 | tf_op jit(solution)/shard_map/all_gather | solution.py:68
  86.4 49.6 %while.10 = (s32[]{:T(128)}, f32[8,128,128]{2,1,0:T(8,128)S(1)}, bf16[8,32]{1,0:T(8,128)(2,1)S(1)}, bf16[8,512,128]{2,1,0:T(8,128)(2,1)}, bf16[32,512,128]{2,1,0...) while((s32[]{:T(128)}, f32[8,128,128]{2,1,0:T(8,128)S(1)}, bf16[8,32]{1,0:T(8,128)(2,1)S(1)}, ...), condition=%wide.region_2.3_spmd, body=%wide.region_1.2_spmd.sunk | while | flops 807403520 | bytes 9765973 | solution.py:57
  86.4 3.0 %fusion.45 = bf16[32,128,128]{2,1,0:T(8,128)(2,1)S(1)} fusion(bf16[32,512,128]{2,1,0:T(8,128)(2,1)} %get-tuple-element.129, bf16[8,512,128]{2,1,0:T(8,128)(2,1)} %get-tuple-element.128, s32[]{:T(128)} %get-tuple-element.118), kind=kOutput, calls=%fused_computation.4.clone.1 | convolution fusion | flops 537395200 | bytes 5374464 | tf_op jit(solution)/shard_map/while/body/eval_jaxpr/ra,crb->cab/dot_general | solution.py:46
  89.4 2.4 %fusion.46 = bf16[32,128,128]{2,1,0:T(8,128)(2,1)S(1)} fusion(bf16[32,128,128]{2,1,0:T(8,128)(2,1)S(1)} %fusion.45, bf16[32,128,128]{2,1,0:T(8,128)(2,1)} %get-tuple-element.130), kind=kOutput, calls=%fused_computation.5.clone.1 | convolution fusion | flops 268959744 | bytes 3145728 | tf_op jit(solution)/shard_map/while/body/eval_jaxpr/cad,ced->cae/dot_general | solution.py:52
  92.5 3.0 %fusion.45 = bf16[32,128,128]{2,1,0:T(8,128)(2,1)S(1)} fusion(bf16[32,512,128]{2,1,0:T(8,128)(2,1)} %get-tuple-element.129, bf16[8,512,128]{2,1,0:T(8,128)(2,1)} %get-tuple-element.128, s32[]{:T(128)} %get-tuple-element.118), kind=kOutput, calls=%fused_computation.4.clone.1 | convolution fusion | flops 537395200 | bytes 5374464 | tf_op jit(solution)/shard_map/while/body/eval_jaxpr/ra,crb->cab/dot_general | solution.py:46
  95.5 2.4 %fusion.46 = bf16[32,128,128]{2,1,0:T(8,128)(2,1)S(1)} fusion(bf16[32,128,128]{2,1,0:T(8,128)(2,1)S(1)} %fusion.45, bf16[32,128,128]{2,1,0:T(8,128)(2,1)} %get-tuple-element.130), kind=kOutput, calls=%fused_computation.5.clone.1 | convolution fusion | flops 268959744 | bytes 3145728 | tf_op jit(solution)/shard_map/while/body/eval_jaxpr/cad,ced->cae/dot_general | solution.py:52
  98.6 3.3 %fusion.45 = bf16[32,128,128]{2,1,0:T(8,128)(2,1)S(1)} fusion(bf16[32,512,128]{2,1,0:T(8,128)(2,1)} %get-tuple-element.129, bf16[8,512,128]{2,1,0:T(8,128)(2,1)} %get-tuple-element.128, s32[]{:T(128)} %get-tuple-element.118), kind=kOutput, calls=%fused_computation.4.clone.1 | convolution fusion | flops 537395200 | bytes 5374464 | tf_op jit(solution)/shard_map/while/body/eval_jaxpr/ra,crb->cab/dot_general | solution.py:46
  101.9 2.4 %fusion.46 = bf16[32,128,128]{2,1,0:T(8,128)(2,1)S(1)} fusion(bf16[32,128,128]{2,1,0:T(8,128)(2,1)S(1)} %fusion.45, bf16[32,128,128]{2,1,0:T(8,128)(2,1)} %get-tuple-element.130), kind=kOutput, calls=%fused_computation.5.clone.1 | convolution fusion | flops 268959744 | bytes 3145728 | tf_op jit(solution)/shard_map/while/body/eval_jaxpr/cad,ced->cae/dot_general | solution.py:52
  105.0 3.1 %fusion.45 = bf16[32,128,128]{2,1,0:T(8,128)(2,1)S(1)} fusion(bf16[32,512,128]{2,1,0:T(8,128)(2,1)} %get-tuple-element.129, bf16[8,512,128]{2,1,0:T(8,128)(2,1)} %get-tuple-element.128, s32[]{:T(128)} %get-tuple-element.118), kind=kOutput, calls=%fused_computation.4.clone.1 | convolution fusion | flops 537395200 | bytes 5374464 | tf_op jit(solution)/shard_map/while/body/eval_jaxpr/ra,crb->cab/dot_general | solution.py:46
  108.1 2.4 %fusion.46 = bf16[32,128,128]{2,1,0:T(8,128)(2,1)S(1)} fusion(bf16[32,128,128]{2,1,0:T(8,128)(2,1)S(1)} %fusion.45, bf16[32,128,128]{2,1,0:T(8,128)(2,1)} %get-tuple-element.130), kind=kOutput, calls=%fused_computation.5.clone.1 | convolution fusion | flops 268959744 | bytes 3145728 | tf_op jit(solution)/shard_map/while/body/eval_jaxpr/cad,ced->cae/dot_general | solution.py:52
  111.2 3.0 %fusion.45 = bf16[32,128,128]{2,1,0:T(8,128)(2,1)S(1)} fusion(bf16[32,512,128]{2,1,0:T(8,128)(2,1)} %get-tuple-element.129, bf16[8,512,128]{2,1,0:T(8,128)(2,1)} %get-tuple-element.128, s32[]{:T(128)} %get-tuple-element.118), kind=kOutput, calls=%fused_computation.4.clone.1 | convolution fusion | flops 537395200 | bytes 5374464 | tf_op jit(solution)/shard_map/while/body/eval_jaxpr/ra,crb->cab/dot_general | solution.py:46
  114.2 2.4 %fusion.46 = bf16[32,128,128]{2,1,0:T(8,128)(2,1)S(1)} fusion(bf16[32,128,128]{2,1,0:T(8,128)(2,1)S(1)} %fusion.45, bf16[32,128,128]{2,1,0:T(8,128)(2,1)} %get-tuple-element.130), kind=kOutput, calls=%fused_computation.5.clone.1 | convolution fusion | flops 268959744 | bytes 3145728 | tf_op jit(solution)/shard_map/while/body/eval_jaxpr/cad,ced->cae/dot_general | solution.py:52
  117.3 3.0 %fusion.45 = bf16[32,128,128]{2,1,0:T(8,128)(2,1)S(1)} fusion(bf16[32,512,128]{2,1,0:T(8,128)(2,1)} %get-tuple-element.129, bf16[8,512,128]{2,1,0:T(8,128)(2,1)} %get-tuple-element.128, s32[]{:T(128)} %get-tuple-element.118), kind=kOutput, calls=%fused_computation.4.clone.1 | convolution fusion | flops 537395200 | bytes 5374464 | tf_op jit(solution)/shard_map/while/body/eval_jaxpr/ra,crb->cab/dot_general | solution.py:46
  120.3 2.4 %fusion.46 = bf16[32,128,128]{2,1,0:T(8,128)(2,1)S(1)} fusion(bf16[32,128,128]{2,1,0:T(8,128)(2,1)S(1)} %fusion.45, bf16[32,128,128]{2,1,0:T(8,128)(2,1)} %get-tuple-element.130), kind=kOutput, calls=%fused_computation.5.clone.1 | convolution fusion | flops 268959744 | bytes 3145728 | tf_op jit(solution)/shard_map/while/body/eval_jaxpr/cad,ced->cae/dot_general | solution.py:52
  123.4 3.1 %fusion.45 = bf16[32,128,128]{2,1,0:T(8,128)(2,1)S(1)} fusion(bf16[32,512,128]{2,1,0:T(8,128)(2,1)} %get-tuple-element.129, bf16[8,512,128]{2,1,0:T(8,128)(2,1)} %get-tuple-element.128, s32[]{:T(128)} %get-tuple-element.118), kind=kOutput, calls=%fused_computation.4.clone.1 | convolution fusion | flops 537395200 | bytes 5374464 | tf_op jit(solution)/shard_map/while/body/eval_jaxpr/ra,crb->cab/dot_general | solution.py:46
  126.5 2.4 %fusion.46 = bf16[32,128,128]{2,1,0:T(8,128)(2,1)S(1)} fusion(bf16[32,128,128]{2,1,0:T(8,128)(2,1)S(1)} %fusion.45, bf16[32,128,128]{2,1,0:T(8,128)(2,1)} %get-tuple-element.130), kind=kOutput, calls=%fused_computation.5.clone.1 | convolution fusion | flops 268959744 | bytes 3145728 | tf_op jit(solution)/shard_map/while/body/eval_jaxpr/cad,ced->cae/dot_general | solution.py:52
  129.6 3.1 %fusion.45 = bf16[32,128,128]{2,1,0:T(8,128)(2,1)S(1)} fusion(bf16[32,512,128]{2,1,0:T(8,128)(2,1)} %get-tuple-element.129, bf16[8,512,128]{2,1,0:T(8,128)(2,1)} %get-tuple-element.128, s32[]{:T(128)} %get-tuple-element.118), kind=kOutput, calls=%fused_computation.4.clone.1 | convolution fusion | flops 537395200 | bytes 5374464 | tf_op jit(solution)/shard_map/while/body/eval_jaxpr/ra,crb->cab/dot_general | solution.py:46
  132.7 2.4 %fusion.46 = bf16[32,128,128]{2,1,0:T(8,128)(2,1)S(1)} fusion(bf16[32,128,128]{2,1,0:T(8,128)(2,1)S(1)} %fusion.45, bf16[32,128,128]{2,1,0:T(8,128)(2,1)} %get-tuple-element.130), kind=kOutput, calls=%fused_computation.5.clone.1 | convolution fusion | flops 268959744 | bytes 3145728 | tf_op jit(solution)/shard_map/while/body/eval_jaxpr/cad,ced->cae/dot_general | solution.py:52
  136.0 26.3 %all-gather.4.cloned.1.call-done = bf16[32,512,512]{2,1,0:T(8,128)(2,1)} async-done(((bf16[1,512,512]{2,1,0:T(8,128)(2,1)}), bf16[32,512,512]{2,1,0:T(8,128)(2,1)}) %all-gather.4.cloned.1.call-update) | async-done | bytes 16777232 | tf_op jit(solution)/shard_map/all_gather | solution.py:72
  162.3 20.3 %fusion.11 = bf16[16,512,512]{2,0,1:T(8,128)(2,1)} fusion(bf16[32,512,512]{2,1,0:T(8,128)(2,1)} %all-gather.4.cloned.1.call-done, s32[16]{0:T(128)S(1)} %select_reduce_fusion), kind=kOutput, calls=%fused_computation.14 | convolution fusion | flops 272630272 | bytes 25165888 | tf_op jit(solution)/shard_map/sk,kxn->sxn/dot_general | solution.py:22
  182.6 11.7 %copy.34 = bf16[16,512,512]{2,1,0:T(8,128)(2,1)} copy(bf16[16,512,512]{2,0,1:T(8,128)(2,1)} %fusion.11) | data formatting | bytes 16777216 | tf_op jit(solution)/shard_map/reshape | solution.py:73
  194.2 5.7 %convolution_convert_fusion.2 = bf16[8,2,512,128]{3,2,1,0:T(8,128)(2,1)S(1)} fusion(bf16[8,2,512,512]{3,2,1,0:T(8,128)(2,1)} %bitcast.55, bf16[8,512,128]{2,1,0:T(8,128)(2,1)S(1)} %copy-done), kind=kOutput, calls=%fused_computation.15 | convolution fusion | flops 1074790400 | bytes 11534336 | tf_op jit(solution)/shard_map/pkxn,pnq->pkxq/dot_general | solution.py:74
  200.0 1.3 fusion.14
  (31 shorter events, 10.9 us)
Async XLA Ops:
  6.5 27.7 %all-gather.8.cloned.1.call-start = ((), (), s32[]{:S(2)}) async-start(), calls=%async_computation.2 | async-start | bytes 1310720 | tf_op jit(solution)/shard_map/all_gather | solution.py:69
  7.3 79.2 %all-gather.6.cloned.1.call-start = ((), (), s32[]{:S(2)}) async-start(), calls=%async_computation.1 | async-start | bytes 5242880 | tf_op jit(solution)/shard_map/all_gather | solution.py:68
  8.0 154.3 %all-gather.4.cloned.1.call-start = ((), (), s32[]{:S(2)}) async-start(), calls=%async_computation | async-start | bytes 17301504 | tf_op jit(solution)/shard_map/all_gather | solution.py:72
  182.6 11.7 %copy-start = (bf16[8,512,128]{2,1,0:T(8,128)(2,1)S(1)}, bf16[8,512,128]{2,1,0:T(8,128)(2,1)}, u32[]{:S(2)}) copy-start(bf16[8,512,128]{2,1,0:T(8,128)(2,1)} %get-tuple-element.140) | copy-start | bytes 3145732
Sparse Core Ops, SparseCore 0:
  9.0 25.2 all-gather.7
  35.9 50.4 all-gather.5
  88.7 73.5 all-gather.3
where the time goes:
time: 208 us
  waiting for transfers between devices  103 us (50%)
  matrix products  77.3 us (37%)
  between operations  13.1 us (6%)
  local copies, waits for them, and re-layouts  12.6 us (6%)
    all_gather x1, waiting for transfers between devices, on_device(): lax.all_gather(domain_bases, 'grp', axis=0, tiled=True)  52.2 us
    all_gather x1, waiting for transfers between devices, on_device(): lax.all_gather(integral_slabs, 'dev', axis=0, tiled=True)  26.3 us
    dot_general x8, matrix products, one_pair(): jnp.einsum('ra,crb->cab', domain_basis, cand_bases, preferred_element_typ...  24.7 us
    all_gather x1, waiting for transfers between devices, on_device(): lax.all_gather(amplitudes, 'grp', axis=0, tiled=True)  22.2 us
    dot_general x1, matrix products, make_fold(): jnp.einsum('sk,kxn->sxn', select, slab_piece, preferred_element_type=jnp....  20.3 us
    dot_general x8, matrix products, one_pair(): jnp.einsum('cad,ced->cae', projected, intersection, preferred_element_typ...  19.1 us
    reshape x1, local copies, waits for them, and re-layouts, on_device(): paired_slabs = side_slabs.reshape(pair_count, 2, naux_full, norb_full)  11.7 us
    dot_general x1, matrix products, on_device(): jnp.einsum('pkxn,pnq->pkxq', paired_slabs, domain_bases, preferred_elemen...  5.71 us
  transfers between devices with their start and end apart: 3, of which 3 were waited for; matrix products, arithmetic and copies ran while one was open for 25% of the time, Pallas kernels for 0%

commit v1 on v0

v1 whole, which is shorter than its diff:
```python
import math

import jax
import jax.numpy as jnp
from jax import lax
from jax.experimental import pallas as pl
from jax.experimental.pallas import tpu as pltpu
from jax.sharding import PartitionSpec as P

NAUX, NORB, NPNO = 512, 512, 128
PDEV, NGRP = 8, 4
RING = 4
HALF = NAUX // 2
QUART = NAUX // 4
MESH = pl.DeviceIdType.MESH
BF16, F32 = jnp.bfloat16, jnp.float32
NT = (((1,), (1,)), ((), ()))
TN = (((0,), (0,)), ((), ()))


def mm(a, b, dims=None):
    if dims is None:
        return jnp.dot(a, b, preferred_element_type=F32)
    return lax.dot_general(a, b, dims, preferred_element_type=F32)


def kernel(
    slab_hbm, u_hbm, t_hbm, cpl_hbm, len_hbm, orb_hbm, owner_hbm, out_ref,
    ubuf, tbuf, meta, cpl, lenv, orbv, lens, orbs, owner, slabs, vbuf, bd, acc, rsend, rin,
    send_sem, y_sem, ym_sem, r_sem, net_sem, sib_sem, loc_sem,
):
    g = lax.axis_index("grp")
    d = lax.axis_index("dev")
    rem, div = lax.rem, lax.div
    c = rem(d, 2)
    x = rem(div(d, 2), RING)
    z = div(d, 2 * RING)
    up, dn = rem(g + 1, NGRP), rem(g + NGRP - 1, NGRP)
    half = rem(g, 2)
    sender2 = div(g, 2) == c
    heavy = div(up, 2) == c

    def dev(zz, xx, cc):
        return rem(zz, RING) * (2 * RING) + rem(xx, RING) * 2 + cc

    def seat(m, o, cc):
        zz = z + (m + (o - m) * c) + RING
        xx = x + (o + (m - o) * c) + RING
        return dev(zz, xx, cc)

    sib = dev(z, x, 1 - c)

    barrier = pltpu.get_barrier_semaphore()
    partners = [(up, d), (dn, d), (g, sib)]
    for dz, dx in ((1, 0), (-1, 0), (0, 1), (0, -1)):
        for cc in (0, 1):
            partners.append((g, dev(z + dz + RING, x + dx + RING, cc)))
    for pg, pd in partners:
        pl.semaphore_signal(barrier, inc=1, device_id=(pg, pd), device_id_type=MESH)


    def local(src, dst, i):
        cp = pltpu.make_async_copy(src, dst, loc_sem.at[i])
        cp.start()
        return cp

    lu = local(u_hbm, ubuf.at[0], 0)
    lt = local(t_hbm, tbuf.at[0], 1)
    lm = [local(cpl_hbm, cpl.at[0], 2), local(len_hbm, lens.at[0], 3)]
    lp = [local(orb_hbm, orbs.at[0], 5), local(owner_hbm, owner, 6)]
    my_rows = slab_hbm.at[pl.ds(half * HALF, HALF), :]
    ls = local(my_rows, slabs.at[d], 4)

    pl.semaphore_wait(barrier, len(partners))

    sent, sent_pred, sent_pred2 = [], [], []
    counter = [0]

    def make(refs, pg, pd):
        i = counter[0]
        counter[0] += 1

        def build():
            src, dst, recv = refs()
            return pltpu.make_async_remote_copy(
                src_ref=src, dst_ref=dst, send_sem=send_sem.at[i], recv_sem=recv,
                device_id=(pg, pd), device_id_type=MESH)
        return build

    def push(src, dst, recv, pg, pd):
        cp = make(lambda: (src, dst, recv), pg, pd)
        cp().start()
        sent.append(cp)

    def arrival(dst, recv):
        pltpu.make_async_remote_copy(
            src_ref=dst, dst_ref=dst, send_sem=send_sem.at[0], recv_sem=recv,
            device_id=(up, d), device_id_type=MESH).wait_recv()

    def y_step(k, row, pg):
        two = pl.ds(2 * k, 2)
        return [
            make(lambda: (u_hbm.at[two], ubuf.at[row, two], y_sem.at[row - 1, k, 0]), pg, d),
            make(lambda: (t_hbm.at[two], tbuf.at[row, two], y_sem.at[row - 1, k, 1]), pg, d),
        ]

    def start_y(k):
        for cp in y_step(k, 1, up):
            cp().start()
            sent.append(cp)

    def quarter(q):
        return slab_hbm.at[pl.ds(half * HALF + q * QUART, QUART), :]

    def slab_dst(s, q):
        return slabs.at[s, pl.ds(q * QUART, QUART), :]

    def y_meta(row, pg):
        return [
            make(lambda: (cpl_hbm, cpl.at[row], ym_sem.at[row - 1, 0]), pg, d),
            make(lambda: (len_hbm, lenv.at[row - 1], ym_sem.at[row - 1, 1]), pg, d),
        ]

    push(orb_hbm, orbv, ym_sem.at[0, 2], up, d)
    for cp in y_meta(1, up):
        cp().start()
        sent.append(cp)
    for k in range(1):
        start_y(k)
    for q, nbrs in ((0, ((0, 1), (0, -1))), (1, ((1, 0), (-1, 0))), (1, ((0, 1), (0, -1))), (0, ((1, 0), (-1, 0)))):
        for dz, dx in nbrs:
            push(quarter(q), slab_dst(d, q), net_sem.at[d], g, dev(z + dz + RING, x + dx + RING, q))
    push(my_rows, slabs.at[d], sib_sem.at[d], g, sib)
    for k in range(1, 4):
        start_y(k)

    @pl.when(sender2)
    def _():
        sent_pred.extend(y_meta(2, dn))
        for k in range(4):
            sent_pred.extend(y_step(k, 2, dn))
        for cp in sent_pred:
            cp().start()

    events = [(0, -1, 0), (0, 1, 1), (0, -1, 1), (0, 1, 0),
              (-1, 0, 0), (1, 0, 1), (-1, 0, 1), (1, 0, 0), (0, 2, 0), (0, 2, 1)]
    for o, k in ((-1, 0), (1, 1), (-1, 1), (1, 0)):
        events += [(-1, o, k), (1, o, k)]
    events += [(2, 0, 0), (2, 0, 1)]
    for o, k in ((2, 0), (2, 1)):
        events += [(-1, o, k), (1, o, k)]
    events += [(2, o, k) for o, k in ((-1, 0), (1, 1), (-1, 1), (1, 0), (2, 0), (2, 1))]
    all_pieces = list(events)

    def relay(n):
        for _ in range(min(n, len(events))):
            m, o, k = events.pop(0)
            s = seat(m, o, k)
            piece = slab_dst(s, c)
            arrival(piece, net_sem.at[s])
            if m == 0:
                if (o, k) == (-1, 0):
                    push(piece, piece, net_sem.at[s], g, seat(0, 1, c))
                if (o, k) == (1, 1):
                    push(piece, piece, net_sem.at[s], g, seat(0, -1, c))
                push(piece, piece, net_sem.at[s], g, seat(1, 0, c))
                push(piece, piece, net_sem.at[s], g, seat(-1, 0, c))
            elif (m, k) == (-1, 0):
                push(piece, piece, net_sem.at[s], g, seat(1, 0, c))
            elif (m, k) == (1, 1):
                push(piece, piece, net_sem.at[s], g, seat(-1, 0, c))
            push(piece, piece, sib_sem.at[s], g, sib)

    def transpose_pairs(row, j):
        for p in (2 * j, 2 * j + 1):
            vbuf[row, p * NPNO:(p + 1) * NPNO, :] = ubuf[row, p].T

    def build_bd(row, j):
        zero = jnp.zeros((NPNO, NPNO), BF16)
        top = jnp.concatenate([tbuf[row, 2 * j], zero], axis=1)
        bot = jnp.concatenate([zero, tbuf[row, 2 * j + 1]], axis=1)
        bd[row, j] = jnp.concatenate([top, bot], axis=0)

    def count(row, cand):
        hit = jnp.sum(jnp.where(meta[row] == cand, 4.0, 0.0), axis=1, keepdims=True)
        return jnp.broadcast_to(hit, (PDEV, NPNO))

    def group_of(row):
        return (g, dn, up)[row]

    def contrib(tgt, lo, n, src, j):
        uq = jnp.concatenate([ubuf[src, 2 * j], ubuf[src, 2 * j + 1]], axis=1)
        bdq = bd[src, j]
        cand = group_of(src) * PDEV + 2 * j
        w = jnp.concatenate([count(tgt, cand), count(tgt, cand + 1)], axis=1)
        for b in range(lo, lo + n, 2):
            rows = slice(b * NPNO, (b + 2) * NPNO)
            s = mm(vbuf[tgt, rows, :], uq).astype(BF16)
            proj = mm(s, bdq)
            for i in (0, 1):
                part = slice(i * NPNO, (i + 1) * NPNO)
                pw = (proj[part] * w[b + i:b + i + 1]).astype(BF16)
                at = slice((b + i) * NPNO, (b + i + 1) * NPNO)
                acc[tgt, at, :] += mm(pw, s[part], NT)

    def loop(n, fn):
        lax.fori_loop(0, n, lambda j, carry: (fn(j), carry)[1], 0)

    def exchange(row, lo, n):
        def one(t):
            i = owner[orbs[row, 0, t]]
            k = owner[orbs[row, 1, t]]
            u = ubuf[row, t]
            left = mm(slabs[i], u).astype(BF16)
            right = mm(slabs[k], u).astype(BF16)
            ex = mm(left, right, TN) * (1.0 / math.sqrt(NAUX))
            at = pl.ds(pl.multiple_of(t * NPNO, NPNO), NPNO)
            acc[row, at, :] += ex
        lax.fori_loop(lo, lo + n, lambda t, carry: (one(t), carry)[1], 0)

    def wait_y(row, k):
        two = pl.ds(2 * k, 2)
        arrival(ubuf.at[row, two], y_sem.at[row - 1, k, 0])
        arrival(tbuf.at[row, two], y_sem.at[row - 1, k, 1])

    def take_meta(row):
        rows = lax.broadcasted_iota(jnp.int32, (PDEV, 32), 0)
        used = jnp.zeros((PDEV, 32), jnp.int32)
        for p in range(PDEV):
            used = jnp.where(rows == p, lens[row, p], used)
        slot = lax.broadcasted_iota(jnp.int32, (PDEV, 32), 1)
        meta[row] = jnp.where(slot < used, cpl[row], -1)

    def arrive_meta(row):
        arrival(cpl.at[row], ym_sem.at[row - 1, 0])
        arrival(lenv.at[row - 1], ym_sem.at[row - 1, 1])
        cp = pltpu.make_async_copy(lenv.at[row - 1], lens.at[row], loc_sem.at[6 + row])
        cp.start()
        cp.wait()
        take_meta(row)

    acc[...] = jnp.zeros_like(acc)
    lu.wait()
    lt.wait()
    for j in range(4):
        transpose_pairs(0, j)
        build_bd(0, j)
    for cp in lm:
        cp.wait()
    take_meta(0)
    relay(4)
    loop(4, lambda j: contrib(0, 0, 8, 0, j))
    relay(6)
    arrive_meta(1)
    arrival(orbv, ym_sem.at[0, 2])
    lp1 = pltpu.make_async_copy(orbv, orbs.at[1], loc_sem.at[9])
    lp1.start()

    def tile1(k):
        wait_y(1, k)
        transpose_pairs(1, k)
        build_bd(1, k)
        contrib(0, 0, 8, 1, k)
        relay(2)
        loop(4, lambda j: contrib(1, 2 * k, 2, 0, j))
        relay(2)

    def tile2(k):
        loop(4, lambda j: contrib(1, 2 * k, 2, 2, j))

    def return1(k):
        two = pl.ds(2 * k, 2)
        rsend[0, 2 * k:2 * k + 2] = acc[1, 2 * k * NPNO:(2 * k + 2) * NPNO, :].astype(BF16).reshape(2, NPNO, NPNO)
        push(rsend.at[0, two], rin.at[0, two], r_sem.at[0, k], dn, d)

    def back2(b):
        two = pl.ds(2 * b, 2)
        return make(lambda: (rsend.at[1, two], rin.at[1, two], r_sem.at[1, b]), up, d)

    tile1(0)
    relay(4)
    tile1(1)
    relay(30)
    tile1(2)

    @pl.when(heavy)
    def _():
        arrive_meta(2)
        for k in range(4):
            wait_y(2, k)
            transpose_pairs(2, k)
            build_bd(2, k)
        for k in range(3):
            contrib(2, 0, 8, 1, k)
            tile2(k)

    ls.wait()
    for cp in lp:
        cp.wait()
    lp1.wait()
    arrival(slabs.at[sib], sib_sem.at[sib])
    for m, o, k in all_pieces:
        s = seat(m, o, k)
        arrival(slab_dst(s, 1 - c), sib_sem.at[s])
    exchange(0, 0, 8)
    exchange(1, 0, 6)
    for k in range(3):
        return1(k)

    tile1(3)

    @pl.when(heavy)
    def _():
        for b in range(4):
            contrib(2, 2 * b, 2, 1, 3)
            rsend[1, 2 * b:2 * b + 2] = acc[2, 2 * b * NPNO:(2 * b + 2) * NPNO, :].astype(BF16).reshape(2, NPNO, NPNO)
            sent_pred2.append(back2(b))
            sent_pred2[-1]().start()
        tile2(3)

    exchange(1, 6, 2)
    return1(3)

    for k in range(4):
        two = pl.ds(2 * k, 2)
        arrival(rin.at[0, two], r_sem.at[0, k])
        mine = acc[0, 2 * k * NPNO:(2 * k + 2) * NPNO, :].reshape(2, NPNO, NPNO)
        out_ref[2 * k:2 * k + 2] = mine + rin[0, 2 * k:2 * k + 2].astype(F32)

    @pl.when(sender2)
    def _():
        for k in range(4):
            two = pl.ds(2 * k, 2)
            arrival(rin.at[1, two], r_sem.at[1, k])
            out_ref[2 * k:2 * k + 2] += rin[1, 2 * k:2 * k + 2].astype(F32)
        for cp in sent_pred:
            cp().wait_send()

    @pl.when(heavy)
    def _():
        for cp in sent_pred2:
            cp().wait_send()

    for cp in sent:
        cp().wait_send()


def on_device(slab, owner, orbs, bases, amps, coupled, coupled_len):
    any_ = pl.BlockSpec(memory_space=pl.ANY)
    dma = pltpu.SemaphoreType.DMA
    return pl.pallas_call(
        kernel,
        out_shape=jax.ShapeDtypeStruct((PDEV, NPNO, NPNO), F32),
        in_specs=[any_] * 7,
        out_specs=pl.BlockSpec(memory_space=pltpu.VMEM),
        scratch_shapes=[
            pltpu.VMEM((3, PDEV, NORB, NPNO), BF16),
            pltpu.VMEM((3, PDEV, NPNO, NPNO), BF16),
            pltpu.VMEM((3, PDEV, 32), jnp.int32),
            pltpu.VMEM((3, PDEV, 32), jnp.int32),
            pltpu.VMEM((2, PDEV), jnp.int32),
            pltpu.VMEM((2, PDEV), jnp.int32),
            pltpu.SMEM((3, PDEV), jnp.int32),
            pltpu.SMEM((2, 2, PDEV), jnp.int32),
            pltpu.SMEM((32,), jnp.int32),
            pltpu.VMEM((32, HALF, NORB), BF16),
            pltpu.VMEM((3, PDEV * NPNO, NORB), BF16),
            pltpu.VMEM((3, 4, 2 * NPNO, 2 * NPNO), BF16),
            pltpu.VMEM((3, PDEV * NPNO, NPNO), F32),
            pltpu.VMEM((2, PDEV, NPNO, NPNO), BF16),
            pltpu.VMEM((2, PDEV, NPNO, NPNO), BF16),
            dma((110,)),
            dma((2, 4, 2)),
            dma((2, 3)),
            dma((2, 4)),
            dma((32,)),
            dma((32,)),
            dma((10,)),
        ],
        compiler_params=pltpu.CompilerParams(
            collective_id=0, has_side_effects=True, vmem_limit_bytes=56 * 1024 * 1024),
        name="residual",
    )(slab[0], bases, amps, coupled, coupled_len, orbs.T, owner)


def solution(mesh):
    pair = ("grp", "dev")
    in_specs = (
        P("dev", None, None), P(), P(pair, None), P(pair, None, None),
        P(pair, None, None), P(pair, None), P(pair),
    )
    return jax.shard_map(
        on_device, mesh=mesh, in_specs=in_specs, out_specs=P(pair, None, None), check_vma=False)
```

time: 208 us -> 67.8 us (0.33)
  waiting for transfers between devices: 103 us -> 0 us
  matrix products: 77.3 us -> 0 us
  Pallas kernels: 0 us -> 64.8 us
  between operations: 13.1 us -> 0.01 us
  local copies, waits for them, and re-layouts: 12.6 us -> 1.87 us
    all_gather x3 -> x0, waiting for transfers between devices: 101 us -> none  [the longest x1 52.2 us: on_device(): lax.all_gather(domain_bases, 'grp', axis=0, tiled=True)]
    dot_general x28 -> x0, matrix products: 77.3 us -> none  [the longest x8 24.7 us: one_pair(): jnp.einsum('ra,crb->cab', domain_basis, cand_bases, preferred_element_typ...]
    pallas_call x0 -> x1, Pallas kernels: none -> 64.8 us  [on_device(): pl.pallas_call(kernel, out_shape=jax.ShapeDtypeStruct((PDEV, NPNO, NPNO),...]
    reshape x1 -> x0, local copies, waits for them, and re-layouts: 11.7 us -> none  [on_device(): paired_slabs = side_slabs.reshape(pair_count, 2, naux_full, norb_full)]
    unnamed x3 -> x0, waiting for transfers between devices: 2.09 us -> none
  transfers between devices with their start and end apart: 3 -> 0, of which waited for: 3 -> 0; matrix products, arithmetic and copies ran while one was open for 25% -> 0% of each run, Pallas kernels for 0% -> 0%
where the time goes in v1:
time: 67.8 us; the launch traced here: 66.7 us
  Pallas kernels  64.8 us (96%)
  local copies, waits for them, and re-layouts  1.87 us (3%)
    pallas_call x1, Pallas kernels, on_device(): pl.pallas_call(kernel, out_shape=jax.ShapeDtypeStruct((PDEV, NPNO, NPNO),...  64.8 us
    unnamed x1, local copies, waits for them, and re-layouts  1.87 us

profile of v1, /device:TPU:1, one launch (start us, length us, event | category | flops | bytes accessed | tf_op | source)
XLA Modules:
  0.0 66.7 jit_solution(12962850590530863484)
XLA Ops:
  0.0 64.8 %residual.1 = f32[8,128,128]{2,1,0:T(8,128)} custom-call(bf16[512,512]{1,0:T(8,128)(2,1)} %bitcast.2, bf16[8,512,128]{2,1,0:T(8,128)(2,1)} %u_hbm.1, bf16[8,128,128]{2,1,0:T(8,128)(2,1)} %t_hbm.1, s32[8,32]{1,0:T(8,128)} %cpl_hbm.1, s32[8]{0:T(128)} %len_hbm.1, s32[2,8]{1,0:T(2,128)} %bitcast.3, s32[32]{0:T(128)} %owner_hbm.1), custom_call_target="tpu_custom_call" | custom-call | tf_op jit(solution)/shard_map/residual/pallas_call | solution.py:351
  64.9 1.9 %copy.9 = f32[8,128,128]{2,1,0:T(8,128)} copy(f32[8,128,128]{2,1,0:T(8,128)} %residual.1) | data formatting | bytes 1048576

commit v2 on v1

--- a/solution.py
+++ b/solution.py
@@ -15,7 +15,6 @@
 MESH = pl.DeviceIdType.MESH
 BF16, F32 = jnp.bfloat16, jnp.float32
 NT = (((1,), (1,)), ((), ()))
-TN = (((0,), (0,)), ((), ()))
 
 
 def mm(a, b, dims=None):
@@ -26,7 +25,7 @@
 
 def kernel(
     slab_hbm, u_hbm, t_hbm, cpl_hbm, len_hbm, orb_hbm, owner_hbm, out_ref,
-    ubuf, tbuf, meta, cpl, lenv, orbv, lens, orbs, owner, slabs, vbuf, bd, acc, rsend, rin,
+    ubuf, tbuf, meta, cpl, lenv, orbv, lens, orbs, owner, slabs, vbuf, bd, acc, halves, rsend, rin,
     send_sem, y_sem, ym_sem, r_sem, net_sem, sib_sem, loc_sem,
 ):
     g = lax.axis_index("grp")
@@ -39,6 +38,7 @@
     half = rem(g, 2)
     sender2 = div(g, 2) == c
     heavy = div(up, 2) == c
+    first = div(rem(up + 1, NGRP), 2) == c
 
     def dev(zz, xx, cc):
         return rem(zz, RING) * (2 * RING) + rem(xx, RING) * 2 + cc
@@ -64,16 +64,16 @@
         cp.start()
         return cp
 
+    my_rows = slab_hbm.at[pl.ds(half * HALF, HALF), :]
+    ls = local(my_rows, slabs.at[d], 4)
     lu = local(u_hbm, ubuf.at[0], 0)
     lt = local(t_hbm, tbuf.at[0], 1)
     lm = [local(cpl_hbm, cpl.at[0], 2), local(len_hbm, lens.at[0], 3)]
     lp = [local(orb_hbm, orbs.at[0], 5), local(owner_hbm, owner, 6)]
-    my_rows = slab_hbm.at[pl.ds(half * HALF, HALF), :]
-    ls = local(my_rows, slabs.at[d], 4)
-
+    ls.wait()
     pl.semaphore_wait(barrier, len(partners))
 
-    sent, sent_pred, sent_pred2 = [], [], []
+    sent, sent_pred = [], []
     counter = [0]
 
     def make(refs, pg, pd):
@@ -104,13 +104,12 @@
             make(lambda: (t_hbm.at[two], tbuf.at[row, two], y_sem.at[row - 1, k, 1]), pg, d),
         ]
 
-    def start_y(k):
-        for cp in y_step(k, 1, up):
+    y_sends = [cp for k in range(4) for cp in y_step(k, 1, up)]
+    sent += y_sends
+
+    def start_y():
+        for cp in y_sends:
             cp().start()
-            sent.append(cp)
-
-    def quarter(q):
-        return slab_hbm.at[pl.ds(half * HALF + q * QUART, QUART), :]
 
     def slab_dst(s, q):
         return slabs.at[s, pl.ds(q * QUART, QUART), :]
@@ -125,14 +124,11 @@
     for cp in y_meta(1, up):
         cp().start()
         sent.append(cp)
-    for k in range(1):
-        start_y(k)
     for q, nbrs in ((0, ((0, 1), (0, -1))), (1, ((1, 0), (-1, 0))), (1, ((0, 1), (0, -1))), (0, ((1, 0), (-1, 0)))):
         for dz, dx in nbrs:
-            push(quarter(q), slab_dst(d, q), net_sem.at[d], g, dev(z + dz + RING, x + dx + RING, q))
-    push(my_rows, slabs.at[d], sib_sem.at[d], g, sib)
-    for k in range(1, 4):
-        start_y(k)
+            push(slab_dst(d, q), slab_dst(d, q), net_sem.at[d], g, dev(z + dz + RING, x + dx + RING, q))
+    push(slabs.at[d], slabs.at[d], sib_sem.at[d], g, sib)
+    pl.when(first)(start_y)
 
     @pl.when(sender2)
     def _():
@@ -173,7 +169,7 @@
 
     def transpose_pairs(row, j):
         for p in (2 * j, 2 * j + 1):
-            vbuf[row, p * NPNO:(p + 1) * NPNO, :] = ubuf[row, p].T
+            vbuf[row, p] = ubuf[row, p].T
 
     def build_bd(row, j):
         zero = jnp.zeros((NPNO, NPNO), BF16)
@@ -194,29 +190,38 @@
         cand = group_of(src) * PDEV + 2 * j
         w = jnp.concatenate([count(tgt, cand), count(tgt, cand + 1)], axis=1)
         for b in range(lo, lo + n, 2):
-            rows = slice(b * NPNO, (b + 2) * NPNO)
-            s = mm(vbuf[tgt, rows, :], uq).astype(BF16)
+            s = mm(vbuf[tgt, b:b + 2].reshape(2 * NPNO, NORB), uq).astype(BF16)
             proj = mm(s, bdq)
             for i in (0, 1):
                 part = slice(i * NPNO, (i + 1) * NPNO)
                 pw = (proj[part] * w[b + i:b + i + 1]).astype(BF16)
-                at = slice((b + i) * NPNO, (b + i + 1) * NPNO)
-                acc[tgt, at, :] += mm(pw, s[part], NT)
+                acc[tgt, b + i] += mm(pw, s[part], NT)
+
+    def contrib_pair(k, src):
+        lo = 2 * k
+        us = jnp.concatenate([ubuf[src, i] for i in range(PDEV)], axis=1)
+        s = mm(vbuf[1, lo:lo + 2].reshape(2 * NPNO, NORB), us).astype(BF16)
+        scaled = []
+        for j in range(4):
+            cand = group_of(src) * PDEV + 2 * j
+            w = jnp.concatenate([count(1, cand), count(1, cand + 1)], axis=1)
+            proj = mm(s[:, j * 256:(j + 1) * 256], bd[src, j])
+            scaled.append([(proj[i * NPNO:(i + 1) * NPNO] * w[lo + i:lo + i + 1]).astype(BF16) for i in (0, 1)])
+        for i in (0, 1):
+            pw = jnp.concatenate([v[i] for v in scaled], axis=1)
+            acc[1, lo + i] += mm(pw, s[i * NPNO:(i + 1) * NPNO], NT)
 
     def loop(n, fn):
         lax.fori_loop(0, n, lambda j, carry: (fn(j), carry)[1], 0)
 
     def exchange(row, lo, n):
-        def one(t):
-            i = owner[orbs[row, 0, t]]
-            k = owner[orbs[row, 1, t]]
-            u = ubuf[row, t]
-            left = mm(slabs[i], u).astype(BF16)
-            right = mm(slabs[k], u).astype(BF16)
-            ex = mm(left, right, TN) * (1.0 / math.sqrt(NAUX))
-            at = pl.ds(pl.multiple_of(t * NPNO, NPNO), NPNO)
-            acc[row, at, :] += ex
-        lax.fori_loop(lo, lo + n, lambda t, carry: (one(t), carry)[1], 0)
+        def half(t, carry):
+            halves[0, t] = mm(vbuf[row, t], slabs[owner[orbs[row, 0, t]]], NT).astype(BF16)
+            halves[1, t] = mm(slabs[owner[orbs[row, 1, t]]], ubuf[row, t]).astype(BF16).T
+            return carry
+        lax.fori_loop(lo, lo + n, half, 0)
+        for t in range(lo, lo + n):
+            acc[row, t] += mm(halves[0, t], halves[1, t], NT) * (1.0 / math.sqrt(NAUX))
 
     def wait_y(row, k):
         two = pl.ds(2 * k, 2)
@@ -251,6 +256,7 @@
     relay(4)
     loop(4, lambda j: contrib(0, 0, 8, 0, j))
     relay(6)
+    pl.when(jnp.logical_not(first))(start_y)
     arrive_meta(1)
     arrival(orbv, ym_sem.at[0, 2])
     lp1 = pltpu.make_async_copy(orbv, orbs.at[1], loc_sem.at[9])
@@ -260,71 +266,87 @@
         wait_y(1, k)
         transpose_pairs(1, k)
         build_bd(1, k)
-        contrib(0, 0, 8, 1, k)
-        relay(2)
-        loop(4, lambda j: contrib(1, 2 * k, 2, 0, j))
-        relay(2)
-
-    def tile2(k):
-        loop(4, lambda j: contrib(1, 2 * k, 2, 2, j))
+        contrib_pair(k, 0)
 
     def return1(k):
         two = pl.ds(2 * k, 2)
-        rsend[0, 2 * k:2 * k + 2] = acc[1, 2 * k * NPNO:(2 * k + 2) * NPNO, :].astype(BF16).reshape(2, NPNO, NPNO)
-        push(rsend.at[0, two], rin.at[0, two], r_sem.at[0, k], dn, d)
-
-    def back2(b):
+        rsend[0, 2 * k:2 * k + 2] = acc[1, 2 * k:2 * k + 2].astype(BF16)
+        return make(lambda: (rsend.at[0, two], rin.at[0, two], r_sem.at[0, k]), dn, d)
+
+    def return2(b):
         two = pl.ds(2 * b, 2)
+        rsend[1, 2 * b:2 * b + 2] = acc[2, 2 * b:2 * b + 2].astype(BF16)
         return make(lambda: (rsend.at[1, two], rin.at[1, two], r_sem.at[1, b]), up, d)
 
-    tile1(0)
-    relay(4)
-    tile1(1)
-    relay(30)
-    tile1(2)
+    def go(cps, cp):
+        cp().start()
+        cps.append(cp)
+
+    def wait_slabs():
+        for cp in lp:
+            cp.wait()
+        lp1.wait()
+        arrival(slabs.at[sib], sib_sem.at[sib])
+        for m, o, k in all_pieces:
+            s = seat(m, o, k)
+            arrival(slab_dst(s, 1 - c), sib_sem.at[s])
+
+    common_sent, common_events, common_count = sent[:], events[:], counter[0]
 
     @pl.when(heavy)
     def _():
+        sent[:], events[:] = [], common_events[:]
+        cps = []
+        for k in range(4):
+            tile1(k)
+            relay(2)
+            contrib(0, 0, 8, 1, k)
+            relay(2)
         arrive_meta(2)
         for k in range(4):
             wait_y(2, k)
             transpose_pairs(2, k)
             build_bd(2, k)
-        for k in range(3):
+        relay(2)
+        for k in range(4):
             contrib(2, 0, 8, 1, k)
-            tile2(k)
-
-    ls.wait()
-    for cp in lp:
-        cp.wait()
-    lp1.wait()
-    arrival(slabs.at[sib], sib_sem.at[sib])
-    for m, o, k in all_pieces:
-        s = seat(m, o, k)
-        arrival(slab_dst(s, 1 - c), sib_sem.at[s])
-    exchange(0, 0, 8)
-    exchange(1, 0, 6)
-    for k in range(3):
-        return1(k)
-
-    tile1(3)
-
-    @pl.when(heavy)
+            relay(1)
+        for b in range(4):
+            go(cps, return2(b))
+        for k in range(4):
+            contrib_pair(k, 2)
+            relay(30 if k == 3 else 1)
+        wait_slabs()
+        exchange(1, 0, 8)
+        for k in range(4):
+            go(cps, return1(k))
+        exchange(0, 0, 8)
+        for cp in cps + sent:
+            cp().wait_send()
+
+    counter[0] = common_count
+
+    @pl.when(jnp.logical_not(heavy))
     def _():
-        for b in range(4):
-            contrib(2, 2 * b, 2, 1, 3)
-            rsend[1, 2 * b:2 * b + 2] = acc[2, 2 * b * NPNO:(2 * b + 2) * NPNO, :].astype(BF16).reshape(2, NPNO, NPNO)
-            sent_pred2.append(back2(b))
-            sent_pred2[-1]().start()
-        tile2(3)
-
-    exchange(1, 6, 2)
-    return1(3)
+        sent[:], events[:] = [], common_events[:]
+        cps = []
+        relay(30)
+        wait_slabs()
+        exchange(0, 0, 8)
+        for k in range(4):
+            tile1(k)
+            exchange(1, 2 * k, 2)
+            go(cps, return1(k))
+            contrib(0, 0, 8, 1, k)
+        for cp in cps + sent:
+            cp().wait_send()
+
+    sent[:] = common_sent
 
     for k in range(4):
         two = pl.ds(2 * k, 2)
         arrival(rin.at[0, two], r_sem.at[0, k])
-        mine = acc[0, 2 * k * NPNO:(2 * k + 2) * NPNO, :].reshape(2, NPNO, NPNO)
+        mine = acc[0, 2 * k:2 * k + 2]
         out_ref[2 * k:2 * k + 2] = mine + rin[0, 2 * k:2 * k + 2].astype(F32)
 
     @pl.when(sender2)
@@ -334,11 +356,6 @@
             arrival(rin.at[1, two], r_sem.at[1, k])
             out_ref[2 * k:2 * k + 2] += rin[1, 2 * k:2 * k + 2].astype(F32)
         for cp in sent_pred:
-            cp().wait_send()
-
-    @pl.when(heavy)
-    def _():
-        for cp in sent_pred2:
             cp().wait_send()
 
     for cp in sent:
@@ -364,9 +381,10 @@
             pltpu.SMEM((2, 2, PDEV), jnp.int32),
             pltpu.SMEM((32,), jnp.int32),
             pltpu.VMEM((32, HALF, NORB), BF16),
-            pltpu.VMEM((3, PDEV * NPNO, NORB), BF16),
+            pltpu.VMEM((3, PDEV, NPNO, NORB), BF16),
             pltpu.VMEM((3, 4, 2 * NPNO, 2 * NPNO), BF16),
-            pltpu.VMEM((3, PDEV * NPNO, NPNO), F32),
+            pltpu.VMEM((3, PDEV, NPNO, NPNO), F32),
+            pltpu.VMEM((2, PDEV, NPNO, HALF), BF16),
             pltpu.VMEM((2, PDEV, NPNO, NPNO), BF16),
             pltpu.VMEM((2, PDEV, NPNO, NPNO), BF16),
             dma((110,)),

time: 67.8 us -> 53.2 us (0.78)
  Pallas kernels: 64.8 us -> 50.3 us
    pallas_call x1, Pallas kernels: 64.8 us -> 50.3 us  [on_device(): pl.pallas_call(kernel, out_shape=jax.ShapeDtypeStruct((PDEV, NPNO, NPNO),...]
where the time goes in v2:
time: 53.2 us; the launch traced here: 52.1 us
  Pallas kernels  50.3 us (95%)
  local copies, waits for them, and re-layouts  1.87 us (4%)
    pallas_call x1, Pallas kernels, on_device(): pl.pallas_call(kernel, out_shape=jax.ShapeDtypeStruct((PDEV, NPNO, NPNO),...  50.3 us
    unnamed x1, local copies, waits for them, and re-layouts  1.87 us

profile of v2, /device:TPU:1, one launch (start us, length us, event | category | flops | bytes accessed | tf_op | source)
XLA Modules:
  0.0 52.1 jit_solution(4600432202435395345)
XLA Ops:
  0.0 50.3 %residual.1 = f32[8,128,128]{2,1,0:T(8,128)} custom-call(bf16[512,512]{1,0:T(8,128)(2,1)} %bitcast.2, bf16[8,512,128]{2,1,0:T(8,128)(2,1)} %u_hbm.1, bf16[8,128,128]{2,1,0:T(8,128)(2,1)} %t_hbm.1, s32[8,32]{1,0:T(8,128)} %cpl_hbm.1, s32[8]{0:T(128)} %len_hbm.1, s32[2,8]{1,0:T(2,128)} %bitcast.3, s32[32]{0:T(128)} %owner_hbm.1), custom_call_target="tpu_custom_call" | custom-call | tf_op jit(solution)/shard_map/residual/pallas_call | solution.py:368
  50.3 1.9 %copy.9 = f32[8,128,128]{2,1,0:T(8,128)} copy(f32[8,128,128]{2,1,0:T(8,128)} %residual.1) | data formatting | bytes 1048576

commit v3 on v2

--- a/solution.py
+++ b/solution.py
@@ -12,8 +12,10 @@
 RING = 4
 HALF = NAUX // 2
 QUART = NAUX // 4
+STEPS = ((0, 2), (2, 2), (4, 2), (6, 1), (7, 1))
 MESH = pl.DeviceIdType.MESH
 BF16, F32 = jnp.bfloat16, jnp.float32
+TN = (((0,), (0,)), ((), ()))
 NT = (((1,), (1,)), ((), ()))
 
 
@@ -24,8 +26,8 @@
 
 
 def kernel(
-    slab_hbm, u_hbm, t_hbm, cpl_hbm, len_hbm, orb_hbm, owner_hbm, out_ref,
-    ubuf, tbuf, meta, cpl, lenv, orbv, lens, orbs, owner, slabs, vbuf, bd, acc, halves, rsend, rin,
+    slab_hbm, u_hbm, t_hbm, cpl_hbm, len_hbm, orb_hbm, owner_hbm, own_out, rin1, rin2,
+    ubuf, tbuf, meta, cpl, lenv, orbv, lens, orbs, owner, slabs, vbuf, bd, acc, halves, rsend,
     send_sem, y_sem, ym_sem, r_sem, net_sem, sib_sem, loc_sem,
 ):
     g = lax.axis_index("grp")
@@ -98,13 +100,13 @@
             device_id=(up, d), device_id_type=MESH).wait_recv()
 
     def y_step(k, row, pg):
-        two = pl.ds(2 * k, 2)
+        two = pl.ds(*STEPS[k])
         return [
             make(lambda: (u_hbm.at[two], ubuf.at[row, two], y_sem.at[row - 1, k, 0]), pg, d),
             make(lambda: (t_hbm.at[two], tbuf.at[row, two], y_sem.at[row - 1, k, 1]), pg, d),
         ]
 
-    y_sends = [cp for k in range(4) for cp in y_step(k, 1, up)]
+    y_sends = [cp for k in range(len(STEPS)) for cp in y_step(k, 1, up)]
     sent += y_sends
 
     def start_y():
@@ -133,7 +135,7 @@
     @pl.when(sender2)
     def _():
         sent_pred.extend(y_meta(2, dn))
-        for k in range(4):
+        for k in range(len(STEPS)):
             sent_pred.extend(y_step(k, 2, dn))
         for cp in sent_pred:
             cp().start()
@@ -167,8 +169,8 @@
                 push(piece, piece, net_sem.at[s], g, seat(-1, 0, c))
             push(piece, piece, sib_sem.at[s], g, sib)
 
-    def transpose_pairs(row, j):
-        for p in (2 * j, 2 * j + 1):
+    def transpose_pairs(row, lo, n):
+        for p in range(lo, lo + n):
             vbuf[row, p] = ubuf[row, p].T
 
     def build_bd(row, j):
@@ -197,17 +199,16 @@
                 pw = (proj[part] * w[b + i:b + i + 1]).astype(BF16)
                 acc[tgt, b + i] += mm(pw, s[part], NT)
 
-    def contrib_pair(k, src):
-        lo = 2 * k
+    def contrib_pair(lo, n, src):
         us = jnp.concatenate([ubuf[src, i] for i in range(PDEV)], axis=1)
-        s = mm(vbuf[1, lo:lo + 2].reshape(2 * NPNO, NORB), us).astype(BF16)
+        s = mm(vbuf[1, lo:lo + n].reshape(n * NPNO, NORB), us).astype(BF16)
         scaled = []
         for j in range(4):
             cand = group_of(src) * PDEV + 2 * j
             w = jnp.concatenate([count(1, cand), count(1, cand + 1)], axis=1)
             proj = mm(s[:, j * 256:(j + 1) * 256], bd[src, j])
-            scaled.append([(proj[i * NPNO:(i + 1) * NPNO] * w[lo + i:lo + i + 1]).astype(BF16) for i in (0, 1)])
-        for i in (0, 1):
+            scaled.append([(proj[i * NPNO:(i + 1) * NPNO] * w[lo + i:lo + i + 1]).astype(BF16) for i in range(n)])
+        for i in range(n):
             pw = jnp.concatenate([v[i] for v in scaled], axis=1)
             acc[1, lo + i] += mm(pw, s[i * NPNO:(i + 1) * NPNO], NT)
 
@@ -215,16 +216,20 @@
         lax.fori_loop(0, n, lambda j, carry: (fn(j), carry)[1], 0)
 
     def exchange(row, lo, n):
-        def half(t, carry):
-            halves[0, t] = mm(vbuf[row, t], slabs[owner[orbs[row, 0, t]]], NT).astype(BF16)
-            halves[1, t] = mm(slabs[owner[orbs[row, 1, t]]], ubuf[row, t]).astype(BF16).T
+        unit = next(v for v in (4, 2, 1) if n % v == 0)
+
+        def half(b, carry):
+            for i in range(unit):
+                t = lo + b * unit + i
+                halves[t, :HALF] = mm(slabs[owner[orbs[row, 0, t]]], ubuf[row, t]).astype(BF16)
+                halves[t, HALF:] = mm(slabs[owner[orbs[row, 1, t]]], ubuf[row, t]).astype(BF16)
             return carry
-        lax.fori_loop(lo, lo + n, half, 0)
+        lax.fori_loop(0, n // unit, half, 0)
         for t in range(lo, lo + n):
-            acc[row, t] += mm(halves[0, t], halves[1, t], NT) * (1.0 / math.sqrt(NAUX))
+            acc[row, t] += mm(halves[t, :HALF], halves[t, HALF:], TN) * (1.0 / math.sqrt(NAUX))
 
     def wait_y(row, k):
-        two = pl.ds(2 * k, 2)
+        two = pl.ds(*STEPS[k])
         arrival(ubuf.at[row, two], y_sem.at[row - 1, k, 0])
         arrival(tbuf.at[row, two], y_sem.at[row - 1, k, 1])
 
@@ -245,38 +250,48 @@
         take_meta(row)
 
     acc[...] = jnp.zeros_like(acc)
+    rsend[1] = jnp.zeros((PDEV, NPNO, NPNO), BF16)
     lu.wait()
     lt.wait()
     for j in range(4):
-        transpose_pairs(0, j)
+        transpose_pairs(0, 2 * j, 2)
         build_bd(0, j)
     for cp in lm:
         cp.wait()
     take_meta(0)
-    relay(4)
     loop(4, lambda j: contrib(0, 0, 8, 0, j))
-    relay(6)
+    relay(12)
     pl.when(jnp.logical_not(first))(start_y)
     arrive_meta(1)
     arrival(orbv, ym_sem.at[0, 2])
-    lp1 = pltpu.make_async_copy(orbv, orbs.at[1], loc_sem.at[9])
+    lp1 = pltpu.make_async_copy(orbv, orbs.at[1], loc_sem.at[10])
     lp1.start()
 
+    def clear():
+        return pltpu.make_async_copy(rsend.at[1], rin2, loc_sem.at[11])
+
+    @pl.when(jnp.logical_not(sender2))
+    def _():
+        clear().start()
+        clear().wait()
+
     def tile1(k):
+        lo, n = STEPS[k]
         wait_y(1, k)
-        transpose_pairs(1, k)
-        build_bd(1, k)
-        contrib_pair(k, 0)
+        transpose_pairs(1, lo, n)
+        if (lo + n) % 2 == 0:
+            build_bd(1, lo // 2)
+        contrib_pair(lo, n, 0)
 
     def return1(k):
-        two = pl.ds(2 * k, 2)
-        rsend[0, 2 * k:2 * k + 2] = acc[1, 2 * k:2 * k + 2].astype(BF16)
-        return make(lambda: (rsend.at[0, two], rin.at[0, two], r_sem.at[0, k]), dn, d)
+        lo, n = STEPS[k]
+        rsend[0, lo:lo + n] = acc[1, lo:lo + n].astype(BF16)
+        return make(lambda: (rsend.at[0, pl.ds(lo, n)], rin1.at[pl.ds(lo, n)], r_sem.at[0, k]), dn, d)
 
     def return2(b):
         two = pl.ds(2 * b, 2)
         rsend[1, 2 * b:2 * b + 2] = acc[2, 2 * b:2 * b + 2].astype(BF16)
-        return make(lambda: (rsend.at[1, two], rin.at[1, two], r_sem.at[1, b]), up, d)
+        return make(lambda: (rsend.at[1, two], rin2.at[two], r_sem.at[1, b]), up, d)
 
     def go(cps, cp):
         cp().start()
@@ -291,36 +306,46 @@
             s = seat(m, o, k)
             arrival(slab_dst(s, 1 - c), sib_sem.at[s])
 
+    def flush():
+        return pltpu.make_async_copy(acc.at[0], own_out, loc_sem.at[9])
+
     common_sent, common_events, common_count = sent[:], events[:], counter[0]
 
     @pl.when(heavy)
     def _():
         sent[:], events[:] = [], common_events[:]
         cps = []
-        for k in range(4):
+        for k in range(5):
             tile1(k)
-            relay(2)
-            contrib(0, 0, 8, 1, k)
-            relay(2)
+            relay((0, 0, 2, 2, 0)[k])
+            if k < 3:
+                contrib(0, 0, 8, 1, k)
+                relay((0, 2, 2)[k])
+        contrib(0, 0, 8, 1, 3)
+        relay(2)
         arrive_meta(2)
-        for k in range(4):
+        for k in range(5):
             wait_y(2, k)
-            transpose_pairs(2, k)
-            build_bd(2, k)
-        relay(2)
+        transpose_pairs(2, 0, PDEV)
+        for j in range(4):
+            build_bd(2, j)
         for k in range(4):
             contrib(2, 0, 8, 1, k)
-            relay(1)
+            relay((2, 0, 2, 0)[k])
         for b in range(4):
             go(cps, return2(b))
         for k in range(4):
-            contrib_pair(k, 2)
-            relay(30 if k == 3 else 1)
+            contrib_pair(2 * k, 2, 2)
+            relay((2, 0, 30, 0)[k])
         wait_slabs()
-        exchange(1, 0, 8)
-        for k in range(4):
+        exchange(1, 0, 4)
+        go(cps, return1(0))
+        go(cps, return1(1))
+        exchange(1, 4, 4)
+        for k in (2, 3, 4):
             go(cps, return1(k))
         exchange(0, 0, 8)
+        flush().start()
         for cp in cps + sent:
             cp().wait_send()
 
@@ -330,31 +355,42 @@
     def _():
         sent[:], events[:] = [], common_events[:]
         cps = []
+        relay(6)
+        tile1(0)
+        relay(4)
+        tile1(1)
         relay(30)
+        contrib(0, 0, 8, 1, 0)
+        contrib(0, 0, 8, 1, 1)
         wait_slabs()
-        exchange(0, 0, 8)
-        for k in range(4):
+        exchange(1, 0, 4)
+        go(cps, return1(0))
+        go(cps, return1(1))
+        exchange(0, 0, 4)
+        tile1(2)
+        exchange(1, 4, 2)
+        go(cps, return1(2))
+        for k in (3, 4):
             tile1(k)
-            exchange(1, 2 * k, 2)
+            exchange(1, STEPS[k][0], 1)
             go(cps, return1(k))
-            contrib(0, 0, 8, 1, k)
+        contrib(0, 0, 8, 1, 2)
+        exchange(0, 4, 4)
+        contrib(0, 0, 8, 1, 3)
+        flush().start()
         for cp in cps + sent:
             cp().wait_send()
 
     sent[:] = common_sent
 
-    for k in range(4):
-        two = pl.ds(2 * k, 2)
-        arrival(rin.at[0, two], r_sem.at[0, k])
-        mine = acc[0, 2 * k:2 * k + 2]
-        out_ref[2 * k:2 * k + 2] = mine + rin[0, 2 * k:2 * k + 2].astype(F32)
+    flush().wait()
+    for k, (lo, n) in enumerate(STEPS):
+        arrival(rin1.at[pl.ds(lo, n)], r_sem.at[0, k])
 
     @pl.when(sender2)
     def _():
         for k in range(4):
-            two = pl.ds(2 * k, 2)
-            arrival(rin.at[1, two], r_sem.at[1, k])
-            out_ref[2 * k:2 * k + 2] += rin[1, 2 * k:2 * k + 2].astype(F32)
+            arrival(rin2.at[pl.ds(2 * k, 2)], r_sem.at[1, k])
         for cp in sent_pred:
             cp().wait_send()
 
@@ -365,11 +401,14 @@
 def on_device(slab, owner, orbs, bases, amps, coupled, coupled_len):
     any_ = pl.BlockSpec(memory_space=pl.ANY)
     dma = pltpu.SemaphoreType.DMA
-    return pl.pallas_call(
+    def shape(t):
+        return jax.ShapeDtypeStruct((PDEV, NPNO, NPNO), t)
+
+    own, back1, back2 = pl.pallas_call(
         kernel,
-        out_shape=jax.ShapeDtypeStruct((PDEV, NPNO, NPNO), F32),
+        out_shape=[shape(F32), shape(BF16), shape(BF16)],
         in_specs=[any_] * 7,
-        out_specs=pl.BlockSpec(memory_space=pltpu.VMEM),
+        out_specs=[any_] * 3,
         scratch_shapes=[
             pltpu.VMEM((3, PDEV, NORB, NPNO), BF16),
             pltpu.VMEM((3, PDEV, NPNO, NPNO), BF16),
@@ -384,21 +423,21 @@
             pltpu.VMEM((3, PDEV, NPNO, NORB), BF16),
             pltpu.VMEM((3, 4, 2 * NPNO, 2 * NPNO), BF16),
             pltpu.VMEM((3, PDEV, NPNO, NPNO), F32),
-            pltpu.VMEM((2, PDEV, NPNO, HALF), BF16),
+            pltpu.VMEM((PDEV, NAUX, NPNO), BF16),
             pltpu.VMEM((2, PDEV, NPNO, NPNO), BF16),
-            pltpu.VMEM((2, PDEV, NPNO, NPNO), BF16),
-            dma((110,)),
-            dma((2, 4, 2)),
+            dma((120,)),
+            dma((2, 5, 2)),
             dma((2, 3)),
-            dma((2, 4)),
+            dma((2, 5)),
             dma((32,)),
             dma((32,)),
-            dma((10,)),
+            dma((12,)),
         ],
         compiler_params=pltpu.CompilerParams(
             collective_id=0, has_side_effects=True, vmem_limit_bytes=56 * 1024 * 1024),
         name="residual",
     )(slab[0], bases, amps, coupled, coupled_len, orbs.T, owner)
+    return own + back1.astype(F32) + back2.astype(F32)
 
 
 def solution(mesh):

time: 53.2 us -> 50.1 us (0.942); the launches traced: 52.1 us -> 49.9 us
  Pallas kernels: 50.3 us -> 47.8 us
  other arithmetic: 0 us -> 2.06 us
  local copies, waits for them, and re-layouts: 1.87 us -> 0 us
    pallas_call x1, Pallas kernels: 50.3 us -> 47.8 us  [on_device(): pl.pallas_call(kernel, out_shape=[shape(F32), shape(BF16), shape(BF16)],...]
    add x0 -> x1, other arithmetic: none -> 2.06 us  [on_device(): return own + back1.astype(F32) + back2.astype(F32)]
    unnamed x1 -> x0, local copies, waits for them, and re-layouts: 1.87 us -> none
where the time goes in v3:
time: 50.1 us; the launch traced here: 49.9 us
  Pallas kernels  47.8 us (95%)
  other arithmetic  2.06 us (4%)
    pallas_call x1, Pallas kernels, on_device(): pl.pallas_call(kernel, out_shape=[shape(F32), shape(BF16), shape(BF16)],...  47.8 us
    add x1, other arithmetic, on_device(): return own + back1.astype(F32) + back2.astype(F32)  2.06 us

profile of v3, /device:TPU:1, one launch (start us, length us, event | category | flops | bytes accessed | tf_op | source)
XLA Modules:
  0.0 49.9 jit_solution(734402071932434316)
XLA Ops:
  0.0 47.8 %residual.1 = (f32[8,128,128]{2,1,0:T(8,128)}, bf16[8,128,128]{2,1,0:T(8,128)(2,1)}, bf16[8,128,128]{2,1,0:T(8,128)(2,1)}) custom-call(bf16[512,512]{1,0:T(8,128)(2,1)} %bitcast.2, bf16[8,512,128]{2,1,0:T(8,128)(2,1)} %u_hbm.1, bf16[8,128,128]{2,1,0:T(8,128)(2,1)} %t_hbm.1, s32[8,32]{1,0:T(8,128)} %cpl_hbm.1, s32[8]{0:T(128)} %len_hbm.1, s32[2,8]{1,0:T(2,128)} %bitcast.3, ...), custom_call_target="tpu_custom_call" | custom-call | tf_op jit(solution)/shard_map/residual/pallas_call | solution.py:407
  47.8 2.1 %convert_add_fusion = f32[8,128,128]{2,1,0:T(8,128)} fusion(bf16[8,128,128]{2,1,0:T(8,128)(2,1)} %get-tuple-element.10, f32[8,128,128]{2,1,0:T(8,128)} %get-tuple-element.8, bf16[8,128,128]{2,1,0:T(8,128)(2,1)} %get-tuple-element.9), kind=kLoop, calls=%fused_computation | loop fusion | flops 524288 | bytes 1572864 | tf_op jit(solution)/shard_map/add | solution.py:440

commit v4 on v3

--- a/solution.py
+++ b/solution.py
@@ -126,10 +126,6 @@
     for cp in y_meta(1, up):
         cp().start()
         sent.append(cp)
-    for q, nbrs in ((0, ((0, 1), (0, -1))), (1, ((1, 0), (-1, 0))), (1, ((0, 1), (0, -1))), (0, ((1, 0), (-1, 0)))):
-        for dz, dx in nbrs:
-            push(slab_dst(d, q), slab_dst(d, q), net_sem.at[d], g, dev(z + dz + RING, x + dx + RING, q))
-    push(slabs.at[d], slabs.at[d], sib_sem.at[d], g, sib)
     pl.when(first)(start_y)
 
     @pl.when(sender2)
@@ -139,6 +135,11 @@
             sent_pred.extend(y_step(k, 2, dn))
         for cp in sent_pred:
             cp().start()
+
+    for q, nbrs in ((0, ((0, 1), (0, -1))), (1, ((1, 0), (-1, 0))), (1, ((0, 1), (0, -1))), (0, ((1, 0), (-1, 0)))):
+        for dz, dx in nbrs:
+            push(slab_dst(d, q), slab_dst(d, q), net_sem.at[d], g, dev(z + dz + RING, x + dx + RING, q))
+    push(slabs.at[d], slabs.at[d], sib_sem.at[d], g, sib)
 
     events = [(0, -1, 0), (0, 1, 1), (0, -1, 1), (0, 1, 0),
               (-1, 0, 0), (1, 0, 1), (-1, 0, 1), (1, 0, 0), (0, 2, 0), (0, 2, 1)]

time: 50.1 us -> 50.1 us (level)
  no operation moved by 1% of the time
where the time goes in v4:
time: 50.1 us; the launch traced here: 49.9 us
  Pallas kernels  47.8 us (95%)
  other arithmetic  2.06 us (4%)
    pallas_call x1, Pallas kernels, on_device(): pl.pallas_call(kernel, out_shape=[shape(F32), shape(BF16), shape(BF16)],...  47.8 us
    add x1, other arithmetic, on_device(): return own + back1.astype(F32) + back2.astype(F32)  2.06 us

profile of v4, /device:TPU:1, one launch (start us, length us, event | category | flops | bytes accessed | tf_op | source)
XLA Modules:
  0.0 49.9 jit_solution(1960156721647212167)
XLA Ops:
  0.0 47.8 %residual.1 = (f32[8,128,128]{2,1,0:T(8,128)}, bf16[8,128,128]{2,1,0:T(8,128)(2,1)}, bf16[8,128,128]{2,1,0:T(8,128)(2,1)}) custom-call(bf16[512,512]{1,0:T(8,128)(2,1)} %bitcast.2, bf16[8,512,128]{2,1,0:T(8,128)(2,1)} %u_hbm.1, bf16[8,128,128]{2,1,0:T(8,128)(2,1)} %t_hbm.1, s32[8,32]{1,0:T(8,128)} %cpl_hbm.1, s32[8]{0:T(128)} %len_hbm.1, s32[2,8]{1,0:T(2,128)} %bitcast.3, ...), custom_call_target="tpu_custom_call" | custom-call | tf_op jit(solution)/shard_map/residual/pallas_call | solution.py:408
  47.8 2.1 %convert_add_fusion = f32[8,128,128]{2,1,0:T(8,128)} fusion(bf16[8,128,128]{2,1,0:T(8,128)(2,1)} %get-tuple-element.10, f32[8,128,128]{2,1,0:T(8,128)} %get-tuple-element.8, bf16[8,128,128]{2,1,0:T(8,128)(2,1)} %get-tuple-element.9), kind=kLoop, calls=%fused_computation | loop fusion | flops 524288 | bytes 1572864 | tf_op jit(solution)/shard_map/add | solution.py:441
